TPU v7x, 32 devices: a whole 2x2x4 slice. The times are simulated.
32 devices in a mesh: groups: 2 (over y), pool: 4 (over z), sub: 2 (over x), chip: 2 (over core).
Axes of the slice: x: 2, y: 2, z: 4, core: 2. Of those that a mesh axis runs over, the one named last changes fastest.
Arguments:
- hidden: bfloat16 [1024, 4096], P(('groups', 'pool', 'sub', 'chip')), parts along dimension 0, may hold values from -6 to 6
- query_weight_matrix: bfloat16 [4096, 4096], P(None, 'pool'), may hold values from -0.09375 to 0.09375
- adapter_down_weight: bfloat16 [64, 64, 4096], P('pool', None, ('sub', 'chip')), may hold values from -0.09375 to 0.09375
- adapter_up_weight: bfloat16 [64, 64, 4096], P('pool', None, ('sub', 'chip')), may hold values from -0.75 to 0.75
- adapter_index_rows: int32 [1024], P(('groups', 'pool', 'sub', 'chip')), parts along dimension 0, may hold values from 0 to 63, as said below
Outputs:
- query: bfloat16 [1024, 4096], P(('groups', 'pool', 'sub', 'chip')), parts along dimension 0
There are 2 independent parts, one for each index of `groups`. A program takes and returns all parts, laid end to end along the dimension named above; an argument that names none is the same for every part. Nothing has to cross between parts.
Inputs may be any that keep to these rules, and one draw needn't show every extreme that they name: A row's owner is adapter_index_rows // 16. In each aligned block of 32 rows (the rows of one device) at most 12 rows have one owner, and in every block some owner has exactly 12 rows.
All inputs are finite; a program needn't handle non-finite values.
Results may differ from a plain program's by a relative error of at most 0.0052.
Values may be sent and summed in bfloat16 or wider, within the bound.
A program may use at most 64 MiB of HBM per device.

v0:
```python
import jax
import jax.numpy as jnp
from jax import lax
from jax.sharding import PartitionSpec as P

ADAPTER_SCALE = 0.5


def owner_rank(owner, count):
    table = (owner[:, None] == jnp.arange(count, dtype=jnp.int32)[None, :]).astype(jnp.int32)
    running = jnp.cumsum(table, axis=0) - table
    return jnp.sum(running * table, axis=1)


def reduced_rank_term(incoming_rows, nearby_adapters, adapter_down_weight, adapter_up_weight):
    adapter_stack, rank_extent, portion_width = adapter_down_weight.shape
    flattened_down = adapter_down_weight.reshape(adapter_stack * rank_extent, portion_width)
    project = lax.dot_general(
        incoming_rows, flattened_down, (((1,), (1,)), ((), ())), preferred_element_type=jnp.float32
    )
    select = nearby_adapters[:, None] == jnp.arange(adapter_stack, dtype=jnp.int32)[None, :]
    partial_low = jnp.sum(
        project.reshape(-1, adapter_stack, rank_extent) * select[:, :, None].astype(jnp.float32),
        axis=1,
    )
    projected_down = lax.psum(partial_low, ("sub", "chip")).astype(jnp.bfloat16)
    spread = (select[:, :, None].astype(jnp.bfloat16) * projected_down[:, None, :]).reshape(
        -1, adapter_stack * rank_extent
    )
    flattened_up = adapter_up_weight.reshape(adapter_stack * rank_extent, portion_width)
    update_term = jnp.dot(spread, flattened_up, preferred_element_type=jnp.float32)
    return (ADAPTER_SCALE * update_term).astype(jnp.bfloat16)


def local(hidden, query_weight_matrix, adapter_down_weight, adapter_up_weight, adapter_index_rows):
    pools = lax.axis_size("pool")
    shards = lax.axis_size(("sub", "chip"))
    shard_index = lax.axis_index(("sub", "chip"))
    row_count, width = hidden.shape
    adapter_stack = adapter_down_weight.shape[0]
    portion_width = adapter_down_weight.shape[2]
    capacity = 2 + row_count // (pools - 1)
    nothing = jnp.zeros((), jnp.bfloat16)
    query_cols = jnp.dot(
        lax.all_gather(hidden, "pool", axis=0, tiled=True),
        query_weight_matrix,
        preferred_element_type=jnp.float32,
    ).astype(jnp.bfloat16)
    block_rows, block_adapters = (
        lax.all_gather(hidden, ("sub", "chip"), axis=0, tiled=True),
        lax.all_gather(adapter_index_rows, ("sub", "chip"), axis=0, tiled=True),
    )
    block_size = shards * row_count
    per_owner = shards * capacity
    combined_output = pools * per_owner
    owner = block_adapters // adapter_stack
    slot = owner * per_owner + owner_rank(owner, pools)
    slot_row = (
        jnp.full((combined_output,), -1, jnp.int32)
        .at[slot]
        .set(jnp.arange(block_size, dtype=jnp.int32))
    )
    filled = slot_row >= 0
    safe_row = jnp.maximum(slot_row, 0)
    my_slice = lax.dynamic_slice_in_dim(block_rows, shard_index * portion_width, portion_width, 1)
    send_rows = jnp.where(filled[:, None], jnp.take(my_slice, safe_row, axis=0), nothing)
    send_adapters = jnp.where(filled, jnp.take(block_adapters % adapter_stack, safe_row), 0)
    received_rows, received_adapters = (
        lax.all_to_all(
            send_rows.reshape(pools, per_owner, portion_width),
            "pool",
            split_axis=0,
            concat_axis=0,
            tiled=True,
        ),
        lax.all_to_all(
            send_adapters.reshape(pools, per_owner), "pool", split_axis=0, concat_axis=0, tiled=True
        ),
    )
    update_term = reduced_rank_term(
        received_rows.reshape(combined_output, portion_width),
        received_adapters.reshape(combined_output),
        adapter_down_weight,
        adapter_up_weight,
    )
    returned = lax.all_to_all(
        update_term.reshape(pools, per_owner, portion_width),
        "pool",
        split_axis=0,
        concat_axis=0,
        tiled=True,
    )
    delta_block = jnp.take(returned.reshape(combined_output, portion_width), slot, axis=0)
    delta_rows = lax.all_to_all(
        delta_block, ("sub", "chip"), split_axis=0, concat_axis=1, tiled=True
    )
    query = lax.all_to_all(query_cols, "pool", split_axis=0, concat_axis=1, tiled=True)
    return (query.astype(jnp.float32) + delta_rows.astype(jnp.float32)).astype(jnp.bfloat16)


def solution(mesh):
    in_specs = (
        P(("groups", "pool", "sub", "chip"), None),
        P(None, "pool"),
        P("pool", None, ("sub", "chip")),
        P("pool", None, ("sub", "chip")),
        P(("groups", "pool", "sub", "chip")),
    )
    out_specs = P(("groups", "pool", "sub", "chip"), None)
    return jax.shard_map(local, mesh=mesh, in_specs=in_specs, out_specs=out_specs, check_vma=False)
```

profile of v0, /device:TPU:0, one launch (start us, length us, event | category | flops | bytes accessed | tf_op | source)
XLA Modules:
  0.0 115.8 jit_solution(494919803565934389)
XLA Ops:
  6.5 0.0 copy-start
  6.5 0.0 all-gather.5.cloned.1.call-start
  6.5 0.7 all-gather.5.cloned.1.call-update
  7.3 1.2 %dynamic-slice = u32[1]{0:T(128)} dynamic-slice(u32[32]{0:T(128)} %constant.102, u32[]{:T(128)S(6)} %add.48), dynamic_slice_sizes={1} | dynamic-slice | bytes 12
  9.2 0.9 dynamic-update-slice
  10.0 6.3 %all-reduce = s32[128]{0:T(128)S(1)} all-reduce(s32[128]{0:T(128)S(1)} %dynamic-update-slice), channel_id=1, replica_groups=mesh['groups'=2,'pool'=4,'sub'=2,'chip'=2] {'sub','chip'}, use_global_device_ids=true, to_apply=%add | all-reduce | flops 128 | bytes 1024
  16.4 0.1 fusion.7
  16.5 0.2 reduce_window_sum.11
  16.7 0.2 select_reduce_fusion
  16.9 1.0 scatter_custom_fusion
  17.9 1.6 %gather_fusion = s32[192]{0:T(256)S(1)} fusion(s32[128]{0:T(128)S(1)} %get-tuple-element.12, s32[1024]{0:T(1024)S(1)} %pad_clamp_fusion.1), kind=kCustom, calls=%fused_computation | custom fusion | bytes 2304 | tf_op jit(solution)/shard_map/jit(_take)/gather | solution.py:67
  19.4 0.7 all_to_all.32
  20.1 4.9 %all-to-all-start.1 = ((s32[4,1,48]{2,1,0:T(1,128)}), s32[4,1,48]{2,1,0:T(1,128)S(1)}, u32[]{:S(2)}, u32[]{:S(2)}) async-start(s32[4,1,48]{2,1,0:T(1,128)} %all_to_all.32), calls=%async_computation.1 | async-start | bytes 4096 | tf_op jit(solution)/shard_map/all_to_all | solution.py:76
  25.0 0.0 all-gather.3.cloned.1.call-start
  25.0 0.7 all-gather.3.cloned.1.call-update
  25.7 0.1 broadcast_in_dim.67
  25.8 0.1 broadcast_in_dim.69
  25.9 2.5 %all-gather.5.cloned.1.call-done = bf16[128,4096]{1,0:T(8,128)(2,1)} async-done(((bf16[32,4096]{1,0:T(8,128)(2,1)}), bf16[128,4096]{1,0:T(8,128)(2,1)}) %all-gather.5.cloned.1.call-update) | async-done | bytes 1048592 | tf_op jit(solution)/shard_map/all_gather | solution.py:50
  28.4 1.0 constant_dynamic-slice_fusion
  29.3 1.0 gather_fusion.1
  30.4 0.9 select_select_fusion
  31.2 0.0 all-to-all-done.1
  31.2 4.6 %all-to-all-start.2 = ((bf16[4,48,1024]{2,1,0:T(8,128)(2,1)}), bf16[4,48,1024]{2,1,0:T(8,128)(2,1)S(1)}, u32[]{:S(2)}, u32[]{:S(2)}) async-start(bf16[4,48,1024]{2,1,0:T(8,128)(2,1)} %select_select_fusion), calls=%async_computation.2 | async-start | bytes 786432 | tf_op jit(solution)/shard_map/all_to_all | solution.py:69
  35.8 0.5 broadcast.96
  36.3 0.7 reduce.3
  37.0 0.1 eq.40
  37.1 20.6 %all-to-all-done.2 = bf16[4,48,1024]{2,1,0:T(8,128)(2,1)S(1)} async-done(((bf16[4,48,1024]{2,1,0:T(8,128)(2,1)}), bf16[4,48,1024]{2,1,0:T(8,128)(2,1)S(1)}, u32[]{:S(2)}, u32[]{:S(2)}) %all-to-all-start.2) | async-done | bytes 393248 | tf_op jit(solution)/shard_map/all_to_all | solution.py:69
  57.7 2.3 %fusion.2 = f32[192,64]{0,1:T(8,128)S(1)} fusion(bf16[192,1024,1]{1,0,2:T(8,128)(2,1)S(1)} %bitcast.27, bf16[16,64,1024]{2,1,0:T(8,128)(2,1)} %param.7, f32[192,16]{0,1:T(8,128)S(1)} %get-tuple-element.11), kind=kOutput, calls=%fused_computation.8 | convolution fusion | flops 403034112 | bytes 2551808 | tf_op jit(solution)/shard_map/dot_general | solution.py:18
  60.1 11.1 %psum.7 = bf16[192,64]{0,1:T(8,128)(2,1)S(1)} all-reduce(f32[192,64]{0,1:T(8,128)S(1)} %fusion.2), channel_id=1, replica_groups=mesh['groups'=2,'pool'=4,'sub'=2,'chip'=2] {'sub','chip'}, use_global_device_ids=true, to_apply=%region_4.5 | all-reduce | flops 12288 | bytes 73728 | tf_op jit(solution)/shard_map/psum | solution.py:26
  71.1 0.0 copy-done
  71.2 1.4 %fusion.1 = bf16[192,1024]{1,0:T(8,128)(2,1)} fusion(bf16[16,64,1024]{2,1,0:T(8,128)(2,1)S(1)} %copy-done, bf16[192,64]{0,1:T(8,128)(2,1)S(1)} %psum.7, bf16[192,16]{0,1:T(8,128)(2,1)S(1)} %get-tuple-element.10), kind=kOutput, calls=%fused_computation.7 | convolution fusion | flops 403243008 | bytes 2521088 | tf_op jit(solution)/shard_map/dot_general | solution.py:31
  72.5 3.5 %all-to-all-start.3 = ((bf16[4,48,1024]{2,1,0:T(8,128)(2,1)}), bf16[4,48,1024]{2,1,0:T(8,128)(2,1)S(1)}, u32[]{:S(2)}, u32[]{:S(2)}) async-start(bf16[4,48,1024]{2,1,0:T(8,128)(2,1)} %bitcast.6), calls=%async_computation.3 | async-start | bytes 786432 | tf_op jit(solution)/shard_map/all_to_all | solution.py:86
  76.0 0.0 all-gather.3.cloned.1.call-done
  76.0 5.7 %convolution_convert_fusion = bf16[128,1024]{1,0:T(8,128)(2,1)} fusion(bf16[128,4096]{1,0:T(8,128)(2,1)} %all-gather.3.cloned.1.call-done, bf16[4096,1024]{1,0:T(8,128)(2,1)} %param.6), kind=kOutput, calls=%fused_computation.9 | convolution fusion | flops 1073872896 | bytes 9699328 | tf_op jit(solution)/shard_map/dot_general | solution.py:44
  81.7 5.7 %all-to-all-done.3 = bf16[4,48,1024]{2,1,0:T(8,128)(2,1)S(1)} async-done(((bf16[4,48,1024]{2,1,0:T(8,128)(2,1)}), bf16[4,48,1024]{2,1,0:T(8,128)(2,1)S(1)}, u32[]{:S(2)}, u32[]{:S(2)}) %all-to-all-start.3) | async-done | bytes 393248 | tf_op jit(solution)/shard_map/all_to_all | solution.py:86
  87.4 3.4 %all-to-all-start = ((bf16[4,32,1024]{2,1,0:T(8,128)(2,1)}), bf16[4,32,1024]{2,1,0:T(8,128)(2,1)S(1)}, u32[]{:S(2)}, u32[]{:S(2)}) async-start(bf16[4,32,1024]{2,1,0:T(8,128)(2,1)} %bitcast), calls=%async_computation | async-start | bytes 524288 | tf_op jit(solution)/shard_map/all_to_all | solution.py:97
  90.8 0.1 broadcast_in_dim.61
  90.9 0.9 gather_fusion.2
  91.7 0.1 broadcast_select_fusion
  91.8 5.7 %all-to-all-done = bf16[4,32,1024]{2,1,0:T(8,128)(2,1)S(1)} async-done(((bf16[4,32,1024]{2,1,0:T(8,128)(2,1)}), bf16[4,32,1024]{2,1,0:T(8,128)(2,1)S(1)}, u32[]{:S(2)}, u32[]{:S(2)}) %all-to-all-start) | async-done | bytes 262176 | tf_op jit(solution)/shard_map/all_to_all | solution.py:97
  97.5 10.6 %all_to_all.42 = bf16[4,32,1024]{2,1,0:T(8,128)(2,1)S(1)} all-to-all(bf16[4,32,1024]{2,1,0:T(8,128)(2,1)S(1)} %broadcast_select_fusion), channel_id=1, replica_groups=mesh['groups'=2,'pool'=4,'sub'=2,'chip'=2] {'sub','chip'}, dimensions={0} | all-to-all | bytes 524288 | tf_op jit(solution)/shard_map/all_to_all | solution.py:94
  108.2 0.1 fusion.4
  108.2 0.7 copy.11
  (9 shorter events, 0.1 us)
Async XLA Ops:
  6.5 64.6 %copy-start = (bf16[16,64,1024]{2,1,0:T(8,128)(2,1)S(1)}, bf16[16,64,1024]{2,1,0:T(8,128)(2,1)}, u32[]{:S(2)}) copy-start(bf16[16,64,1024]{2,1,0:T(8,128)(2,1)} %param.8) | copy-start | bytes 6291460
  6.5 21.8 %all-gather.5.cloned.1.call-start = ((), (), s32[]{:S(2)}) async-start(), calls=%async_computation.6 | async-start | bytes 1310720 | tf_op jit(solution)/shard_map/all_gather | solution.py:50
  20.1 11.1 %all-to-all-start.1 = ((s32[4,1,48]{2,1,0:T(1,128)}), s32[4,1,48]{2,1,0:T(1,128)S(1)}, u32[]{:S(2)}, u32[]{:S(2)}) async-start(s32[4,1,48]{2,1,0:T(1,128)} %all_to_all.32), calls=%async_computation.1 | async-start | bytes 4096 | tf_op jit(solution)/shard_map/all_to_all | solution.py:76
  25.0 51.0 %all-gather.3.cloned.1.call-start = ((), (), s32[]{:S(2)}) async-start(), calls=%async_computation.5 | async-start | bytes 1310720 | tf_op jit(solution)/shard_map/all_gather | solution.py:45
  31.2 26.5 %all-to-all-start.2 = ((bf16[4,48,1024]{2,1,0:T(8,128)(2,1)}), bf16[4,48,1024]{2,1,0:T(8,128)(2,1)S(1)}, u32[]{:S(2)}, u32[]{:S(2)}) async-start(bf16[4,48,1024]{2,1,0:T(8,128)(2,1)} %select_select_fusion), calls=%async_computation.2 | async-start | bytes 786432 | tf_op jit(solution)/shard_map/all_to_all | solution.py:69
  72.5 14.8 %all-to-all-start.3 = ((bf16[4,48,1024]{2,1,0:T(8,128)(2,1)}), bf16[4,48,1024]{2,1,0:T(8,128)(2,1)S(1)}, u32[]{:S(2)}, u32[]{:S(2)}) async-start(bf16[4,48,1024]{2,1,0:T(8,128)(2,1)} %bitcast.6), calls=%async_computation.3 | async-start | bytes 786432 | tf_op jit(solution)/shard_map/all_to_all | solution.py:86
  87.4 10.2 %all-to-all-start = ((bf16[4,32,1024]{2,1,0:T(8,128)(2,1)}), bf16[4,32,1024]{2,1,0:T(8,128)(2,1)S(1)}, u32[]{:S(2)}, u32[]{:S(2)}) async-start(bf16[4,32,1024]{2,1,0:T(8,128)(2,1)} %bitcast), calls=%async_computation | async-start | bytes 524288 | tf_op jit(solution)/shard_map/all_to_all | solution.py:97
Sparse Core Ops, SparseCore 0:
  8.9 19.4 all-gather.4
  29.9 35.1 all-gather.2
where the time goes:
time: 116 us
  waiting for transfers between devices  35.9 us (31%)
  blocking collectives  28.1 us (24%)
  starting transfers between devices  16.3 us (14%)
  between operations  14.2 us (12%)
  local copies, waits for them, and re-layouts  9.72 us (8%)
  matrix products  9.37 us (8%)
  other arithmetic  2.18 us (2%)
    all_to_all x1, waiting for transfers between devices, local(): lax.all_to_all(send_rows.reshape(pools, per_owner, portion_width), 'pool'...  20.6 us
    psum x1, blocking collectives, reduced_rank_term(): projected_down = lax.psum(partial_low, ('sub', 'chip')).astype(jnp.bfloat16)  11.1 us
    all_to_all x1, blocking collectives, local(): lax.all_to_all(delta_block, ('sub', 'chip'), split_axis=0, concat_axis=1,...  10.6 us
    unnamed x1, blocking collectives  6.35 us
    all_to_all x1, waiting for transfers between devices, local(): lax.all_to_all(query_cols, 'pool', split_axis=0, concat_axis=1, tiled=True)  5.69 us
    dot_general x1, matrix products, local(): jnp.dot(lax.all_gather(hidden, 'pool', axis=0, tiled=True), query_weight_...  5.68 us
    all_to_all x1, waiting for transfers between devices, local(): lax.all_to_all(update_term.reshape(pools, per_owner, portion_width), 'poo...  5.67 us
    all_to_all x1, starting transfers between devices, local(): lax.all_to_all(send_adapters.reshape(pools, per_owner), 'pool', split_axi...  4.87 us
  transfers between devices with their start and end apart: 6, of which 4 were waited for; matrix products, arithmetic and copies ran while one was open for 17% of the time, Pallas kernels for 0%

commit v1 on v0

--- a/solution.py
+++ b/solution.py
@@ -4,6 +4,17 @@
 from jax.sharding import PartitionSpec as P
 
 ADAPTER_SCALE = 0.5
+
+
+def in_blocks(value, dim, peers):
+    before, after = (value.shape[:dim], value.shape[dim + 1 :])
+    return jnp.moveaxis(value.reshape(*before, peers, -1, *after), dim, 0)
+
+
+def joined_along(blocks, dim):
+    blocks = jnp.moveaxis(blocks, 0, dim)
+    dims = blocks.shape
+    return blocks.reshape(*dims[:dim], dims[dim] * dims[dim + 1], *dims[dim + 2 :])
 
 
 def owner_rank(owner, count):
@@ -94,7 +105,16 @@
     delta_rows = lax.all_to_all(
         delta_block, ("sub", "chip"), split_axis=0, concat_axis=1, tiled=True
     )
-    query = lax.all_to_all(query_cols, "pool", split_axis=0, concat_axis=1, tiled=True)
+    count_2, index = (lax.axis_size("pool"), lax.axis_index("pool"))
+    blocks = in_blocks(query_cols, 0, count_2)
+    finished = [blocks[index]]
+    for step in range(1, count_2):
+        sent = blocks[(index + step) % count_2]
+        finished.append(
+            lax.ppermute(sent, "pool", [(i, (i + step) % count_2) for i in range(count_2)])
+        )
+    blocks = jnp.stack(finished)[(index - jnp.arange(count_2)) % count_2]
+    query = joined_along(blocks, 1)
     return (query.astype(jnp.float32) + delta_rows.astype(jnp.float32)).astype(jnp.bfloat16)
 
 

time: 116 us -> 110 us (0.948)
  blocking collectives: 28.1 us -> 17.4 us
  starting transfers between devices: 16.3 us -> 21.3 us
    all_to_all x1 -> x0, blocking collectives: 10.6 us -> none  [local(): lax.all_to_all(delta_block, ('sub', 'chip'), split_axis=0, concat_axis=1,...]
    ppermute x0 -> x3, starting transfers between devices: none -> 4.94 us  [local(): lax.ppermute(sent, 'pool', [(i, (i + step) % count_2) for i in range(coun...]
  transfers between devices with their start and end apart: 6 -> 9, of which waited for: 4 -> 4; matrix products, arithmetic and copies ran while one was open for 17% -> 19% of each run, Pallas kernels for 0% -> 0%
where the time goes in v1:
time: 110 us
  waiting for transfers between devices  35.1 us (32%)
  starting transfers between devices  21.3 us (19%)
  blocking collectives  17.4 us (16%)
  between operations  14.3 us (13%)
  local copies, waits for them, and re-layouts  10.3 us (9%)
  matrix products  8.69 us (8%)
  other arithmetic  2.95 us (3%)
    all_to_all x1, waiting for transfers between devices, local(): lax.all_to_all(send_rows.reshape(pools, per_owner, portion_width), 'pool'...  20.5 us
    psum x1, blocking collectives, reduced_rank_term(): projected_down = lax.psum(partial_low, ('sub', 'chip')).astype(jnp.bfloat16)  11.1 us
    unnamed x1, blocking collectives  6.35 us
    all_to_all x1, waiting for transfers between devices, local(): lax.all_to_all(delta_block, ('sub', 'chip'), split_axis=0, concat_axis=1,...  5.34 us
    all_to_all x1, waiting for transfers between devices, local(): lax.all_to_all(update_term.reshape(pools, per_owner, portion_width), 'poo...  5.28 us
    dot_general x1, matrix products, local(): jnp.dot(lax.all_gather(hidden, 'pool', axis=0, tiled=True), query_weight_...  4.97 us
    ppermute x3, starting transfers between devices, local(): lax.ppermute(sent, 'pool', [(i, (i + step) % count_2) for i in range(coun...  4.94 us
    all_to_all x1, starting transfers between devices, local(): lax.all_to_all(send_adapters.reshape(pools, per_owner), 'pool', split_axi...  4.87 us
  transfers between devices with their start and end apart: 9, of which 4 were waited for; matrix products, arithmetic and copies ran while one was open for 19% of the time, Pallas kernels for 0%

profile of v1, /device:TPU:0, one launch (start us, length us, event | category | flops | bytes accessed | tf_op | source)
XLA Modules:
  0.0 110.0 jit_solution(9752463077464793776)
XLA Ops:
  6.5 0.0 copy-start
  6.5 0.0 all-gather.5.cloned.1.call-start
  6.5 0.7 all-gather.5.cloned.1.call-update
  7.3 1.2 %dynamic-slice = u32[1]{0:T(128)} dynamic-slice(u32[32]{0:T(128)} %constant.138, u32[]{:T(128)S(6)} %add.114), dynamic_slice_sizes={1} | dynamic-slice | bytes 12
  9.2 0.9 dynamic-update-slice
  10.0 6.3 %all-reduce = s32[128]{0:T(128)S(1)} all-reduce(s32[128]{0:T(128)S(1)} %dynamic-update-slice), channel_id=1, replica_groups=mesh['groups'=2,'pool'=4,'sub'=2,'chip'=2] {'sub','chip'}, use_global_device_ids=true, to_apply=%add | all-reduce | flops 128 | bytes 1024
  16.4 0.1 fusion.7
  16.5 0.2 reduce_window_sum.11
  16.7 0.2 select_reduce_fusion
  16.9 1.0 scatter_custom_fusion
  17.9 1.6 %gather_fusion.1 = s32[192]{0:T(256)S(1)} fusion(s32[128]{0:T(128)S(1)} %get-tuple-element.16, s32[1024]{0:T(1024)S(1)} %pad_clamp_fusion.1), kind=kCustom, calls=%fused_computation.1 | custom fusion | bytes 2304 | tf_op jit(solution)/shard_map/jit(_take)/gather | solution.py:78
  19.4 0.7 all_to_all.20
  20.1 4.9 %all-to-all-start = ((s32[4,1,48]{2,1,0:T(1,128)}), s32[4,1,48]{2,1,0:T(1,128)S(1)}, u32[]{:S(2)}, u32[]{:S(2)}) async-start(s32[4,1,48]{2,1,0:T(1,128)} %all_to_all.20), calls=%async_computation | async-start | bytes 4096 | tf_op jit(solution)/shard_map/all_to_all | solution.py:87
  25.0 0.0 all-gather.3.cloned.1.call-start
  25.0 0.7 all-gather.3.cloned.1.call-update
  25.7 0.1 broadcast_in_dim.70
  25.8 0.1 broadcast_in_dim.68
  25.9 2.5 %all-gather.5.cloned.1.call-done = bf16[128,4096]{1,0:T(8,128)(2,1)} async-done(((bf16[32,4096]{1,0:T(8,128)(2,1)}), bf16[128,4096]{1,0:T(8,128)(2,1)}) %all-gather.5.cloned.1.call-update) | async-done | bytes 1048592 | tf_op jit(solution)/shard_map/all_gather | solution.py:61
  28.4 1.0 constant_dynamic-slice_fusion
  29.3 1.0 gather_fusion.2
  30.4 0.9 select_select_fusion
  31.2 0.0 all-to-all-done
  31.2 4.6 %all-to-all-start.1 = ((bf16[4,48,1024]{2,1,0:T(8,128)(2,1)}), bf16[4,48,1024]{2,1,0:T(8,128)(2,1)S(1)}, u32[]{:S(2)}, u32[]{:S(2)}) async-start(bf16[4,48,1024]{2,1,0:T(8,128)(2,1)} %select_select_fusion), calls=%async_computation.1 | async-start | bytes 786432 | tf_op jit(solution)/shard_map/all_to_all | solution.py:80
  35.8 0.1 broadcast_in_dim.62
  36.0 0.5 broadcast.172
  36.5 0.7 reduce.3
  37.1 0.1 eq.46
  37.2 20.5 %all-to-all-done.1 = bf16[4,48,1024]{2,1,0:T(8,128)(2,1)S(1)} async-done(((bf16[4,48,1024]{2,1,0:T(8,128)(2,1)}), bf16[4,48,1024]{2,1,0:T(8,128)(2,1)S(1)}, u32[]{:S(2)}, u32[]{:S(2)}) %all-to-all-start.1) | async-done | bytes 393248 | tf_op jit(solution)/shard_map/all_to_all | solution.py:80
  57.7 2.3 %fusion.2 = f32[192,64]{0,1:T(8,128)S(1)} fusion(bf16[192,1024,1]{1,0,2:T(8,128)(2,1)S(1)} %bitcast.39, bf16[16,64,1024]{2,1,0:T(8,128)(2,1)} %param.7, f32[192,16]{0,1:T(8,128)S(1)} %get-tuple-element.15), kind=kOutput, calls=%fused_computation.9 | convolution fusion | flops 403034112 | bytes 2551808 | tf_op jit(solution)/shard_map/dot_general | solution.py:29
  60.1 11.1 %psum.7 = bf16[192,64]{0,1:T(8,128)(2,1)S(1)} all-reduce(f32[192,64]{0,1:T(8,128)S(1)} %fusion.2), channel_id=1, replica_groups=mesh['groups'=2,'pool'=4,'sub'=2,'chip'=2] {'sub','chip'}, use_global_device_ids=true, to_apply=%region_4.5 | all-reduce | flops 12288 | bytes 73728 | tf_op jit(solution)/shard_map/psum | solution.py:37
  71.2 1.4 %fusion.1 = bf16[192,1024]{1,0:T(8,128)(2,1)} fusion(bf16[16,64,1024]{2,1,0:T(8,128)(2,1)S(1)} %copy-done, bf16[192,64]{0,1:T(8,128)(2,1)S(1)} %psum.7, bf16[192,16]{0,1:T(8,128)(2,1)S(1)} %get-tuple-element.14), kind=kOutput, calls=%fused_computation.8 | convolution fusion | flops 403243008 | bytes 2521088 | tf_op jit(solution)/shard_map/dot_general | solution.py:42
  72.5 3.5 %all-to-all-start.2 = ((bf16[4,48,1024]{2,1,0:T(8,128)(2,1)}), bf16[4,48,1024]{2,1,0:T(8,128)(2,1)S(1)}, u32[]{:S(2)}, u32[]{:S(2)}) async-start(bf16[4,48,1024]{2,1,0:T(8,128)(2,1)} %bitcast.13), calls=%async_computation.2 | async-start | bytes 786432 | tf_op jit(solution)/shard_map/all_to_all | solution.py:97
  76.0 0.0 all-gather.3.cloned.1.call-done
  76.0 5.0 %convolution_convert_fusion = bf16[128,1024]{1,0:T(8,128)(2,1)S(1)} fusion(bf16[128,4096]{1,0:T(8,128)(2,1)} %all-gather.3.cloned.1.call-done, bf16[4096,1024]{1,0:T(8,128)(2,1)} %param.6), kind=kOutput, calls=%fused_computation.10 | convolution fusion | flops 1073872896 | bytes 9699328 | tf_op jit(solution)/shard_map/dot_general | solution.py:55
  81.1 3.8 %collective-permute-start.2 = (bf16[32,1024]{1,0:T(8,128)(2,1)S(1)}, bf16[32,1024]{1,0:T(8,128)(2,1)S(1)}, u32[]{:S(2)}, u32[]{:S(2)}) collective-permute-start(bf16[32,1024]{1,0:T(8,128)(2,1)S(1)} %get-tuple-element.11), channel_id=1, source_target_pairs={{0,12},{4,0},{8,4},{12,8},{1,13},{5,1},{9,5},{13,9},{2,14},{6,2},{... | collective-permute-start | bytes 196616 | tf_op jit(solution)/shard_map/ppermute | solution.py:114
  84.9 0.0 collective-permute-start.1
  84.9 1.1 %collective-permute-start = (bf16[32,1024]{1,0:T(8,128)(2,1)S(1)}, bf16[32,1024]{1,0:T(8,128)(2,1)S(1)}, u32[]{:S(2)}, u32[]{:S(2)}) collective-permute-start(bf16[32,1024]{1,0:T(8,128)(2,1)S(1)} %get-tuple-element.13), channel_id=1, source_target_pairs={{0,4},{4,8},{8,12},{12,0},{1,5},{5,9},{9,13},{13,1},{2,6},{6,10},{... | collective-permute-start | bytes 196616 | tf_op jit(solution)/shard_map/ppermute | solution.py:114
  86.0 5.3 %all-to-all-done.2 = bf16[4,48,1024]{2,1,0:T(8,128)(2,1)S(1)} async-done(((bf16[4,48,1024]{2,1,0:T(8,128)(2,1)}), bf16[4,48,1024]{2,1,0:T(8,128)(2,1)S(1)}, u32[]{:S(2)}, u32[]{:S(2)}) %all-to-all-start.2) | async-done | bytes 393248 | tf_op jit(solution)/shard_map/all_to_all | solution.py:97
  91.3 0.9 gather_fusion.3
  92.1 0.8 broadcast_select_fusion
  92.9 3.4 %all-to-all-start.3 = ((bf16[4,32,1024]{2,1,0:T(8,128)(2,1)}), bf16[4,32,1024]{2,1,0:T(8,128)(2,1)S(1)}, u32[]{:S(2)}, u32[]{:S(2)}) async-start(bf16[4,32,1024]{2,1,0:T(8,128)(2,1)} %broadcast_select_fusion), calls=%async_computation.3 | async-start | bytes 524288 | tf_op jit(solution)/shard_map/all_to_all | solution.py:105
  96.4 0.0 collective-permute-done.2
  96.4 0.0 collective-permute-done.1
  96.4 0.0 collective-permute-done
  96.4 0.6 gather_fusion
  97.0 5.3 %all-to-all-done.3 = bf16[4,32,1024]{2,1,0:T(8,128)(2,1)S(1)} async-done(((bf16[4,32,1024]{2,1,0:T(8,128)(2,1)}), bf16[4,32,1024]{2,1,0:T(8,128)(2,1)S(1)}, u32[]{:S(2)}, u32[]{:S(2)}) %all-to-all-start.3) | async-done | bytes 262176 | tf_op jit(solution)/shard_map/all_to_all | solution.py:105
  102.4 0.1 fusion.4
  102.4 0.7 copy.11
  (14 shorter events, 0.1 us)
Async XLA Ops:
  6.5 64.6 %copy-start = (bf16[16,64,1024]{2,1,0:T(8,128)(2,1)S(1)}, bf16[16,64,1024]{2,1,0:T(8,128)(2,1)}, u32[]{:S(2)}) copy-start(bf16[16,64,1024]{2,1,0:T(8,128)(2,1)} %param.8) | copy-start | bytes 6291460
  6.5 21.8 %all-gather.5.cloned.1.call-start = ((), (), s32[]{:S(2)}) async-start(), calls=%async_computation.5 | async-start | bytes 1310720 | tf_op jit(solution)/shard_map/all_gather | solution.py:61
  20.1 11.1 %all-to-all-start = ((s32[4,1,48]{2,1,0:T(1,128)}), s32[4,1,48]{2,1,0:T(1,128)S(1)}, u32[]{:S(2)}, u32[]{:S(2)}) async-start(s32[4,1,48]{2,1,0:T(1,128)} %all_to_all.20), calls=%async_computation | async-start | bytes 4096 | tf_op jit(solution)/shard_map/all_to_all | solution.py:87
  25.0 51.1 %all-gather.3.cloned.1.call-start = ((), (), s32[]{:S(2)}) async-start(), calls=%async_computation.4 | async-start | bytes 1310720 | tf_op jit(solution)/shard_map/all_gather | solution.py:56
  31.2 26.5 %all-to-all-start.1 = ((bf16[4,48,1024]{2,1,0:T(8,128)(2,1)}), bf16[4,48,1024]{2,1,0:T(8,128)(2,1)S(1)}, u32[]{:S(2)}, u32[]{:S(2)}) async-start(bf16[4,48,1024]{2,1,0:T(8,128)(2,1)} %select_select_fusion), calls=%async_computation.1 | async-start | bytes 786432 | tf_op jit(solution)/shard_map/all_to_all | solution.py:80
  72.5 18.7 %all-to-all-start.2 = ((bf16[4,48,1024]{2,1,0:T(8,128)(2,1)}), bf16[4,48,1024]{2,1,0:T(8,128)(2,1)S(1)}, u32[]{:S(2)}, u32[]{:S(2)}) async-start(bf16[4,48,1024]{2,1,0:T(8,128)(2,1)} %bitcast.13), calls=%async_computation.2 | async-start | bytes 786432 | tf_op jit(solution)/shard_map/all_to_all | solution.py:97
  81.1 15.3 %collective-permute-start.2 = (bf16[32,1024]{1,0:T(8,128)(2,1)S(1)}, bf16[32,1024]{1,0:T(8,128)(2,1)S(1)}, u32[]{:S(2)}, u32[]{:S(2)}) collective-permute-start(bf16[32,1024]{1,0:T(8,128)(2,1)S(1)} %get-tuple-element.11), channel_id=1, source_target_pairs={{0,12},{4,0},{8,4},{12,8},{1,13},{5,1},{9,5},{13,9},{2,14},{6,2},{... | collective-permute-start | bytes 196616 | tf_op jit(solution)/shard_map/ppermute | solution.py:114
  84.9 11.5 %collective-permute-start.1 = (bf16[32,1024]{1,0:T(8,128)(2,1)S(1)}, bf16[32,1024]{1,0:T(8,128)(2,1)S(1)}, u32[]{:S(2)}, u32[]{:S(2)}) collective-permute-start(bf16[32,1024]{1,0:T(8,128)(2,1)S(1)} %get-tuple-element.12), channel_id=1, source_target_pairs={{0,8},{4,12},{8,0},{12,4},{1,9},{5,13},{9,1},{13,5},{2,10},{6,14},... | collective-permute-start | bytes 196616 | tf_op jit(solution)/shard_map/ppermute | solution.py:114
  84.9 11.5 %collective-permute-start = (bf16[32,1024]{1,0:T(8,128)(2,1)S(1)}, bf16[32,1024]{1,0:T(8,128)(2,1)S(1)}, u32[]{:S(2)}, u32[]{:S(2)}) collective-permute-start(bf16[32,1024]{1,0:T(8,128)(2,1)S(1)} %get-tuple-element.13), channel_id=1, source_target_pairs={{0,4},{4,8},{8,12},{12,0},{1,5},{5,9},{9,13},{13,1},{2,6},{6,10},{... | collective-permute-start | bytes 196616 | tf_op jit(solution)/shard_map/ppermute | solution.py:114
  92.9 9.4 %all-to-all-start.3 = ((bf16[4,32,1024]{2,1,0:T(8,128)(2,1)}), bf16[4,32,1024]{2,1,0:T(8,128)(2,1)S(1)}, u32[]{:S(2)}, u32[]{:S(2)}) async-start(bf16[4,32,1024]{2,1,0:T(8,128)(2,1)} %broadcast_select_fusion), calls=%async_computation.3 | async-start | bytes 524288 | tf_op jit(solution)/shard_map/all_to_all | solution.py:105
Sparse Core Ops, SparseCore 0:
  8.9 19.4 all-gather.4
  29.9 35.1 all-gather.2
